TPU v7x, 128 devices: a whole 4x4x4 slice. The times are simulated.
128 devices in a mesh: tile: 16 (over x_lo, z, core), chan: 8 (over y, x_hi).
Axes of the slice: x: 4 (x_hi: 2, x_lo: 2; x = x_hi * 2 + x_lo), y: 4, z: 4, core: 2. Of those that a mesh axis runs over, the one named last changes fastest.
Arguments:
- voltages: int32 [512, 262144], P('tile', 'chan'), may hold values from -128 to 127
- history: int32 [512, 30720], P('tile'), may hold values from -128 to 127
- filter_taps: int32 [16, 2048], replicated, may hold values from -64 to 64
Outputs:
- visibilities: float32 [2, 1024, 512, 512], P(None, 'chan', 'tile')
Inputs may be any that keep to these rules, and one draw needn't show every extreme that they name: `voltages`: 8-bit signed samples. `history`: 8-bit signed samples.
All inputs are finite; a program needn't handle non-finite values.
Results may differ from a plain program's by a relative error of at most 0.006.
Values may be sent and summed in bfloat16 or wider, within the bound.
A program may use at most 192 MiB of HBM per device.

v0:
```python
import math
import jax
import jax.numpy as jnp
from jax import lax
from jax.sharding import PartitionSpec as P

CH = 1024
TAPS = 16
FFT = 2048
filter_norm = 1.0 / 16384.0


def from_behind(value, axis, steps):
    count = lax.axis_size(axis)
    leading, last = (max(0, -steps), min(count, count - steps))
    return lax.ppermute(value, axis, [(source, source + steps) for source in range(leading, last)])


def dft_table(samples, channels):
    rows_index = jnp.arange(samples, dtype=jnp.int32)[:, None]
    cols_index = jnp.arange(channels, dtype=jnp.int32)[None, :]
    angles = (rows_index * cols_index % samples).astype(jnp.float32) * (2.0 * math.pi / samples)
    factor = 1.0 / math.sqrt(channels)
    return jnp.concatenate([jnp.cos(angles) * factor, -jnp.sin(angles) * factor], axis=1).astype(
        jnp.bfloat16
    )


def polyphase(extended, weights, spectra_count):
    summed = jnp.zeros((extended.shape[0], spectra_count, extended.shape[2]), jnp.float32)
    for tap_index in range(weights.shape[0]):
        summed = (
            summed
            + weights[tap_index][None, None, :]
            * extended[:, tap_index : tap_index + spectra_count, :]
        )
    return summed


def counter_rows(spectra):
    real_part = spectra[:, :, 0]
    imag_part = spectra[:, :, 1]
    rotated = jnp.stack([imag_part, -real_part], axis=2)
    return jnp.stack([spectra, rotated], axis=0)


def body(voltages, history, filter_taps):
    local_inputs = voltages.shape[0]
    spectra_count = voltages.shape[1] // FFT
    tail_blocks = voltages[:, (spectra_count - TAPS + 1) * FFT :].astype(jnp.bfloat16)
    carried = from_behind(tail_blocks, "chan", 1)
    is_first = lax.axis_index("chan") == 0
    earlier = jnp.where(is_first, history.astype(jnp.float32), carried.astype(jnp.float32))
    extended = jnp.concatenate([earlier, voltages.astype(jnp.float32)], axis=1)
    extended = extended.reshape(local_inputs, spectra_count + TAPS - 1, FFT)
    filtered = (
        polyphase(extended, filter_taps.astype(jnp.float32), spectra_count) * filter_norm
    ).astype(jnp.bfloat16)
    spectra = jnp.dot(
        filtered.reshape(-1, FFT), dft_table(FFT, CH), preferred_element_type=jnp.float32
    )
    spectra = spectra.reshape(local_inputs, spectra_count, 2, CH).astype(jnp.bfloat16)
    turned = lax.all_to_all(spectra, "chan", split_axis=3, concat_axis=1, tiled=True)
    total_spectra = turned.shape[1]
    average = 1.0 / total_spectra
    row_sets = counter_rows(turned)
    return (
        jnp.einsum(
            "qaspc,bspc->qcab",
            row_sets,
            lax.all_gather(turned, "tile", axis=0, tiled=True),
            preferred_element_type=jnp.float32,
        )
        * average
    )


def solution(mesh):
    in_specs = (P("tile", "chan"), P("tile", None), P())
    out_specs = P(None, "chan", "tile", None)
    return jax.shard_map(body, mesh=mesh, in_specs=in_specs, out_specs=out_specs, check_vma=False)
```

profile of v0, /device:TPU:1, one launch (start us, length us, event | category | flops | bytes accessed | tf_op | source)
XLA Modules:
  0.0 409.3 jit_solution(11984337973401259222)
XLA Ops:
  6.5 3.7 slice_convert_fusion
  10.3 5.6 %collective-permute-start = (bf16[32,30720]{1,0:T(8,128)(2,1)}, bf16[32,30720]{1,0:T(8,128)(2,1)S(1)}, u32[]{:S(2)}, u32[]{:S(2)}) collective-permute-start(bf16[32,30720]{1,0:T(8,128)(2,1)} %slice_convert_fusion), channel_id=1, source_target_pairs={{0,1},{1,2},{2,3},{3,4},{4,5},{5,6},{6,7},{8,9},{9,10},{10,11},{11... | collective-permute-start | bytes 5898248 | tf_op jit(solution)/shard_map/ppermute | solution.py:16
  15.9 0.1 fusion.40
  16.0 2.2 convert_element_type.28
  18.2 34.9 %multiply_convert_fusion = (bf16[2048,1024]{0,1:T(8,128)(2,1)}, bf16[2048,1024]{0,1:T(8,128)(2,1)}) fusion(), kind=kLoop, calls=%fused_computation.11 | loop fusion | flops 39845888 | bytes 8388608 | tf_op jit(solution)/shard_map/convert.1
  53.2 8.5 %pad_maximum_fusion = bf16[2048,2048]{0,1:T(8,128)(2,1)} fusion(bf16[2048,1024]{0,1:T(8,128)(2,1)} %get-tuple-element.23, bf16[2048,1024]{0,1:T(8,128)(2,1)} %get-tuple-element.24), kind=kLoop, calls=%fused_computation.10 | loop fusion | flops 16777216 | bytes 16777216 | tf_op jit(solution)/shard_map/concatenate | solution.py:24
  61.7 2.6 convert_select_fusion
  64.4 0.7 copy-done
  65.1 3.7 pad_maximum_fusion.1
  68.7 7.6 %reshape.25 = f32[32,31,2048]{2,1,0:T(8,128)} reshape(f32[32,63488]{1,0:T(8,128)} %pad_maximum_fusion.1) | data formatting | bytes 16252928 | tf_op jit(solution)/shard_map/reshape | solution.py:55
  76.4 43.5 %fusion.34 = bf16[32,16,2,1024]{3,1,2,0:T(8,128)(2,1)S(1)} fusion(bf16[2,1024,2048,1]{2,1,0,3:T(8,128)(2,1)} %bitcast.59, f32[32,31,2048]{2,1,0:T(8,128)} %reshape.25, f32[2048]{0:T(1024)S(1)} %bitcast.61, f32[2048]{0:T(1024)S(1)} %bitcast.62, f32[2048]{0:T(1024)S(1)} %bitcast.63, f32[2048]{0:T(1024)S(1)} %bitcast.64, f32[2048]{0:T(1024)S(1)} %bitcast.65, ...), kind=kOutput, calls=%fused_computation.58 | convolution fusion | flops 4330618880 | bytes 77725696 | tf_op jit(solution)/shard_map/dot_general | solution.py:59
  119.9 12.8 %copy.28 = bf16[32,16,2,1024]{0,1,2,3:T(8,128)(2,1)} copy(bf16[32,16,2,1024]{3,1,2,0:T(8,128)(2,1)S(1)} %fusion.34) | data formatting | bytes 4194304 | tf_op jit(solution)/shard_map/convert_element_type | solution.py:62
  132.7 10.1 %reshape.30 = bf16[8,2,65536]{2,1,0:T(2,128)(2,1)S(1)} reshape(bf16[1024,2,16,32]{3,2,1,0:T(8,128)(2,1)} %bitcast.55) | data formatting | bytes 4194304
  142.9 31.9 %all_to_all.18 = bf16[8,2,65536]{2,1,0:T(2,128)(2,1)} all-to-all(bf16[8,2,65536]{2,1,0:T(2,128)(2,1)S(1)} %reshape.30), channel_id=1, replica_groups=mesh['tile'=16,'chan'=8] {'chan'}, dimensions={0} | all-to-all | bytes 4194304 | tf_op jit(solution)/shard_map/all_to_all | solution.py:63
  174.8 8.6 %reshape.31 = bf16[1024,2,16,32]{3,2,1,0:T(8,128)(2,1)} reshape(bf16[8,2,65536]{2,1,0:T(2,128)(2,1)} %all_to_all.18) | data formatting | bytes 4194304
  183.4 10.3 %copy.30 = bf16[32,8,16,2,128]{4,2,1,3,0:T(8,128)(2,1)S(1)} copy(bf16[32,8,16,2,128]{0,2,3,4,1:T(8,128)(2,1)} %bitcast.56) | data formatting | bytes 4194304 | tf_op jit(solution)/shard_map/all_to_all | solution.py:63
  193.7 2.9 copy.31
  196.6 0.0 all-gather.2.cloned.1.call-update
  196.6 3.0 copy.35
  199.6 1.9 fusion.39
  201.5 1.5 maximum_bitcast_fusion
  203.1 165.1 %all-gather.2.cloned.1.call-done = bf16[512,128,2,128]{1,0,2,3:T(8,128)(2,1)} async-done(((bf16[32,128,2,128]{1,0,2,3:T(8,128)(2,1)}), bf16[512,128,2,128]{1,0,2,3:T(8,128)(2,1)}) %all-gather.2.cloned.1.call-update) | async-done | bytes 33554448 | tf_op jit(solution)/shard_map/all_gather | solution.py:71
  368.1 21.9 %fusion.2 = f32[2,128,32,512]{3,2,0,1:T(8,128)} fusion(bf16[512,128,2,128]{1,0,2,3:T(8,128)(2,1)} %all-gather.2.cloned.1.call-done, bf16[1,32,128,2,128]{2,1,3,0,4:T(8,128)(2,1)} %maximum_bitcast_fusion, bf16[1,32,128,2,128]{2,1,3,0,4:T(8,128)(2,1)S(1)} %copy-done.2), kind=kOutput, calls=%fused_computation.3 | convolution fusion | flops 2160066560 | bytes 54525952 | tf_op jit(solution)/shard_map/qaspc,bspc->qcab/dot_general | solution.py:68
  390.1 12.4 %copy.36 = f32[2,128,32,512]{3,2,1,0:T(8,128)} copy(f32[2,128,32,512]{3,2,0,1:T(8,128)} %fusion.2) | data formatting | bytes 33554432 | tf_op jit(solution)/shard_map/mul | solution.py:68
  (10 shorter events, 0.0 us)
Async XLA Ops:
  6.5 9.3 %copy-start.3 = (s32[16,2048]{1,0:T(8,128)S(1)}, s32[16,2048]{1,0:T(8,128)}, u32[]{:S(2)}) copy-start(s32[16,2048]{1,0:T(8,128)} %param.5) | copy-start | bytes 393220
  6.5 361.6 %all-gather.2.cloned.1.call-start = ((), (), s32[]{:S(2)}) async-start(), calls=%async_computation.1 | async-start | bytes 35651584 | tf_op jit(solution)/shard_map/all_gather | solution.py:71
  6.5 9.5 %copy-start.1 = (s32[32,32768]{1,0:T(8,128)S(1)}, s32[32,32768]{1,0:T(8,128)}, u32[]{:S(2)}) copy-start(s32[32,32768]{1,0:T(8,128)} %param.3) | copy-start | bytes 12582916
  10.3 51.4 %collective-permute-start = (bf16[32,30720]{1,0:T(8,128)(2,1)}, bf16[32,30720]{1,0:T(8,128)(2,1)S(1)}, u32[]{:S(2)}, u32[]{:S(2)}) collective-permute-start(bf16[32,30720]{1,0:T(8,128)(2,1)} %slice_convert_fusion), channel_id=1, source_target_pairs={{0,1},{1,2},{2,3},{3,4},{4,5},{5,6},{6,7},{8,9},{9,10},{10,11},{11... | collective-permute-start | bytes 5898248 | tf_op jit(solution)/shard_map/ppermute | solution.py:16
  61.7 3.4 copy-start
  199.6 168.5 %copy-start.2 = (bf16[1,32,128,2,128]{2,1,3,0,4:T(8,128)(2,1)S(1)}, bf16[1,32,128,2,128]{2,1,3,0,4:T(8,128)(2,1)}, u32[]{:S(2)}) copy-start(bf16[1,32,128,2,128]{2,1,3,0,4:T(8,128)(2,1)} %copy.35) | copy-start | bytes 6291460
Sparse Core Ops, SparseCore 0:
  196.8 171.3 all-gather.1
where the time goes:
time: 410 us; the launch traced here: 409 us
  waiting for transfers between devices  165 us (40%)
  local copies, waits for them, and re-layouts  68.6 us (17%)
  matrix products  65.5 us (16%)
  other arithmetic  59.2 us (14%)
  blocking collectives  31.9 us (8%)
  between operations  13.5 us (3%)
  starting transfers between devices  5.58 us (1%)
    all_gather x1, waiting for transfers between devices, body(): lax.all_gather(turned, 'tile', axis=0, tiled=True)  165 us
    dot_general x1, matrix products, body(): jnp.dot(filtered.reshape(-1, FFT), dft_table(FFT, CH), preferred_element_...  43.5 us
    another operation x2, other arithmetic  38.7 us
    all_to_all x1, blocking collectives, body(): lax.all_to_all(spectra, 'chan', split_axis=3, concat_axis=1, tiled=True)  31.9 us
    dot_general x1, matrix products, body(): jnp.einsum('qaspc,bspc->qcab', row_sets, lax.all_gather(turned, 'tile', a...  21.9 us
    unnamed x10, local copies, waits for them, and re-layouts  19.5 us
    all_to_all x2, local copies, waits for them, and re-layouts, body(): lax.all_to_all(spectra, 'chan', split_axis=3, concat_axis=1, tiled=True)  13.2 us
    convert_element_type x1, local copies, waits for them, and re-layouts, body(): spectra.reshape(local_inputs, spectra_count, 2, CH).astype(jnp.bfloat16)  12.8 us
  transfers between devices with their start and end apart: 2, of which 1 were waited for; matrix products, arithmetic and copies ran while one was open for 13% of the time, Pallas kernels for 0%

commit v1 on v0

--- a/solution.py
+++ b/solution.py
@@ -60,7 +60,10 @@
         filtered.reshape(-1, FFT), dft_table(FFT, CH), preferred_element_type=jnp.float32
     )
     spectra = spectra.reshape(local_inputs, spectra_count, 2, CH).astype(jnp.bfloat16)
-    turned = lax.all_to_all(spectra, "chan", split_axis=3, concat_axis=1, tiled=True)
+    turned = jnp.concatenate(
+        lax.all_to_all(jnp.stack(jnp.split(spectra, lax.axis_size("chan"), axis=3)), "chan", 0, 0),
+        axis=1,
+    )
     total_spectra = turned.shape[1]
     average = 1.0 / total_spectra
     row_sets = counter_rows(turned)

time: 410 us -> 370 us (0.902)
  local copies, waits for them, and re-layouts: 68.6 us -> 31.1 us
    unnamed x10 -> x19, local copies, waits for them, and re-layouts: 19.5 us -> 2.68 us
    all_to_all x2 -> x0, local copies, waits for them, and re-layouts: 13.2 us -> none  [body(): lax.all_to_all(spectra, 'chan', split_axis=3, concat_axis=1, tiled=True)]
    convert_element_type x1 -> x0, local copies, waits for them, and re-layouts: 12.8 us -> none  [body(): spectra.reshape(local_inputs, spectra_count, 2, CH).astype(jnp.bfloat16)]
  transfers between devices with their start and end apart: 2 -> 2, of which waited for: 1 -> 1; matrix products, arithmetic and copies ran while one was open for 13% -> 14% of each run, Pallas kernels for 0% -> 0%
where the time goes in v1:
time: 370 us
  waiting for transfers between devices  165 us (45%)
  matrix products  65 us (18%)
  other arithmetic  57.5 us (16%)
  blocking collectives  31.8 us (9%)
  local copies, waits for them, and re-layouts  31.1 us (8%)
  between operations  13.5 us (4%)
  starting transfers between devices  5.58 us (2%)
    all_gather x1, waiting for transfers between devices, body(): lax.all_gather(turned, 'tile', axis=0, tiled=True)  165 us
    dot_general x1, matrix products, body(): jnp.dot(filtered.reshape(-1, FFT), dft_table(FFT, CH), preferred_element_...  43.1 us
    another operation x2, other arithmetic  38.7 us
    all_to_all x1, blocking collectives, body(): lax.all_to_all(jnp.stack(jnp.split(spectra, lax.axis_size('chan'), axis=3...  31.8 us
    dot_general x1, matrix products, body(): jnp.einsum('qaspc,bspc->qcab', row_sets, lax.all_gather(turned, 'tile', a...  22 us
    mul x1, local copies, waits for them, and re-layouts, body(): jnp.einsum('qaspc,bspc->qcab', row_sets, lax.all_gather(turned, 'tile', a...  12.4 us
    concatenate x1, other arithmetic, dft_table(): jnp.concatenate([jnp.cos(angles) * factor, -jnp.sin(angles) * factor], ax...  8.53 us
    reshape x1, local copies, waits for them, and re-layouts, body(): extended = extended.reshape(local_inputs, spectra_count + TAPS - 1, FFT)  7.63 us
  transfers between devices with their start and end apart: 2, of which 1 were waited for; matrix products, arithmetic and copies ran while one was open for 14% of the time, Pallas kernels for 0%

profile of v1, /device:TPU:1, one launch (start us, length us, event | category | flops | bytes accessed | tf_op | source)
XLA Modules:
  0.0 369.6 jit_solution(14210460006169016203)
XLA Ops:
  6.5 3.8 %slice_convert_fusion = bf16[32,30720]{1,0:T(8,128)(2,1)} fusion(s32[32,32768]{1,0:T(8,128)} %param.3), kind=kLoop, calls=%fused_computation.53 | loop fusion | flops 983040 | bytes 5898240 | tf_op jit(solution)/shard_map/convert.2
  10.3 5.6 %collective-permute-start = (bf16[32,30720]{1,0:T(8,128)(2,1)}, bf16[32,30720]{1,0:T(8,128)(2,1)S(1)}, u32[]{:S(2)}, u32[]{:S(2)}) collective-permute-start(bf16[32,30720]{1,0:T(8,128)(2,1)} %slice_convert_fusion), channel_id=1, source_target_pairs={{0,1},{1,2},{2,3},{3,4},{4,5},{5,6},{6,7},{8,9},{9,10},{10,11},{11... | collective-permute-start | bytes 5898248 | tf_op jit(solution)/shard_map/ppermute | solution.py:16
  15.9 0.1 fusion.48
  16.0 2.2 convert_element_type.28
  18.2 34.9 %multiply_convert_fusion = (bf16[2048,1024]{0,1:T(8,128)(2,1)}, bf16[2048,1024]{0,1:T(8,128)(2,1)}) fusion(), kind=kLoop, calls=%fused_computation.11 | loop fusion | flops 39845888 | bytes 8388608 | tf_op jit(solution)/shard_map/convert.1
  53.2 8.5 %pad_maximum_fusion = bf16[2048,2048]{0,1:T(8,128)(2,1)} fusion(bf16[2048,1024]{0,1:T(8,128)(2,1)} %get-tuple-element.23, bf16[2048,1024]{0,1:T(8,128)(2,1)} %get-tuple-element.24), kind=kLoop, calls=%fused_computation.10 | loop fusion | flops 16777216 | bytes 16777216 | tf_op jit(solution)/shard_map/concatenate | solution.py:24
  61.7 2.6 convert_select_fusion
  64.4 0.7 copy-done.2
  65.1 3.7 pad_maximum_fusion.1
  68.7 7.6 %reshape.30 = f32[32,31,2048]{2,1,0:T(8,128)} reshape(f32[32,63488]{1,0:T(8,128)} %pad_maximum_fusion.1) | data formatting | bytes 16252928 | tf_op jit(solution)/shard_map/reshape | solution.py:55
  76.4 43.1 %fusion.34 = bf16[32,16,2,1024]{3,1,2,0:T(8,128)(2,1)S(1)} fusion(bf16[2,1024,2048,1]{2,1,0,3:T(8,128)(2,1)} %bitcast.82, f32[32,31,2048]{2,1,0:T(8,128)} %reshape.30, f32[2048]{0:T(1024)S(1)} %bitcast.85, f32[2048]{0:T(1024)S(1)} %bitcast.86, f32[2048]{0:T(1024)S(1)} %bitcast.87, f32[2048]{0:T(1024)S(1)} %bitcast.88, f32[2048]{0:T(1024)S(1)} %bitcast.89, ...), kind=kOutput, calls=%fused_computation.58 | convolution fusion | flops 4330618880 | bytes 77725696 | tf_op jit(solution)/shard_map/dot_general | solution.py:59
  119.7 0.1 fusion.41
  119.8 0.1 fusion.40
  120.1 0.1 fusion.37
  120.2 31.8 %all_to_all.5 = bf16[8,32,16,2,128]{4,2,3,1,0:T(8,128)(2,1)S(1)} all-to-all(bf16[8,32,16,2,128]{4,2,3,1,0:T(8,128)(2,1)S(1)} %fusion.37), channel_id=1, replica_groups=mesh['tile'=16,'chan'=8] {'chan'}, dimensions={0} | all-to-all | bytes 4194304 | tf_op jit(solution)/shard_map/all_to_all | solution.py:64
  152.0 0.6 copy.5
  152.7 1.3 copy-done.1
  154.0 2.9 copy.6
  156.9 4.8 %copy.10 = bf16[1,32,128,2,128]{2,1,3,0,4:T(8,128)(2,1)} copy(bf16[1,32,128,2,128]{4,2,3,1,0:T(8,128)(2,1)} %bitcast.81) | data formatting | bytes 4194304 | tf_op jit(solution)/shard_map/stack;reshape | solution.py:44
  161.7 0.2 fusion.47
  161.9 1.5 maximum_bitcast_fusion
  163.4 165.0 %all-gather.2.cloned.1.call-done = bf16[512,128,2,128]{1,0,2,3:T(8,128)(2,1)} async-done(((bf16[32,128,2,128]{1,0,2,3:T(8,128)(2,1)}), bf16[512,128,2,128]{1,0,2,3:T(8,128)(2,1)}) %all-gather.2.cloned.1.call-update) | async-done | bytes 33554448 | tf_op jit(solution)/shard_map/all_gather | solution.py:74
  328.4 22.0 %fusion.2 = f32[2,128,32,512]{3,2,0,1:T(8,128)} fusion(bf16[512,128,2,128]{1,0,2,3:T(8,128)(2,1)} %all-gather.2.cloned.1.call-done, bf16[1,32,128,2,128]{2,1,3,0,4:T(8,128)(2,1)} %maximum_bitcast_fusion, bf16[1,32,128,2,128]{2,1,3,0,4:T(8,128)(2,1)S(1)} %copy-done.4), kind=kOutput, calls=%fused_computation.3 | convolution fusion | flops 2160066560 | bytes 54525952 | tf_op jit(solution)/shard_map/qaspc,bspc->qcab/dot_general | solution.py:71
  350.3 12.4 %copy.11 = f32[2,128,32,512]{3,2,1,0:T(8,128)} copy(f32[2,128,32,512]{3,2,0,1:T(8,128)} %fusion.2) | data formatting | bytes 33554432 | tf_op jit(solution)/shard_map/mul | solution.py:71
  (19 shorter events, 0.5 us)
Async XLA Ops:
  6.5 9.3 %copy-start.5 = (s32[16,2048]{1,0:T(8,128)S(1)}, s32[16,2048]{1,0:T(8,128)}, u32[]{:S(2)}) copy-start(s32[16,2048]{1,0:T(8,128)} %param.5) | copy-start | bytes 393220
  6.5 321.8 %all-gather.2.cloned.1.call-start = ((), (), s32[]{:S(2)}) async-start(), calls=%async_computation.1 | async-start | bytes 35651584 | tf_op jit(solution)/shard_map/all_gather | solution.py:74
  6.5 9.5 %copy-start.3 = (s32[32,32768]{1,0:T(8,128)S(1)}, s32[32,32768]{1,0:T(8,128)}, u32[]{:S(2)}) copy-start(s32[32,32768]{1,0:T(8,128)} %param.3) | copy-start | bytes 12582916
  10.3 51.4 %collective-permute-start = (bf16[32,30720]{1,0:T(8,128)(2,1)}, bf16[32,30720]{1,0:T(8,128)(2,1)S(1)}, u32[]{:S(2)}, u32[]{:S(2)}) collective-permute-start(bf16[32,30720]{1,0:T(8,128)(2,1)} %slice_convert_fusion), channel_id=1, source_target_pairs={{0,1},{1,2},{2,3},{3,4},{4,5},{5,6},{6,7},{8,9},{9,10},{10,11},{11... | collective-permute-start | bytes 5898248 | tf_op jit(solution)/shard_map/ppermute | solution.py:16
  61.7 3.4 copy-start.2
  152.6 1.3 copy-start.1
  156.9 4.8 %copy-start = (bf16[32,128,2,128]{1,0,2,3:T(8,128)(2,1)S(1)}, bf16[32,128,2,128]{1,0,2,3:T(8,128)(2,1)}, u32[]{:S(2)}) copy-start(bf16[32,128,2,128]{1,0,2,3:T(8,128)(2,1)} %copy.6) | copy-start | bytes 6291460
  161.9 166.5 %copy-start.4 = (bf16[1,32,128,2,128]{2,1,3,0,4:T(8,128)(2,1)S(1)}, bf16[1,32,128,2,128]{2,1,3,0,4:T(8,128)(2,1)}, u32[]{:S(2)}) copy-start(bf16[1,32,128,2,128]{2,1,3,0,4:T(8,128)(2,1)} %copy.10) | copy-start | bytes 6291460
Sparse Core Ops, SparseCore 0:
  157.0 171.3 all-gather.1
